TPU v7x, 32 devices: a whole 2x2x4 slice. The times are simulated.
32 devices in a mesh: seq: 8 (over z, y), head: 4 (over x, core).
Axes of the slice: x: 2, y: 2, z: 4, core: 2. Of those that a mesh axis runs over, the one named last changes fastest.
Arguments:
- q_latent: bfloat16 [1024, 32, 576], P('seq', 'head'), may hold values from -6 to 6
- kv_latent: bfloat16 [1024, 576], P('seq'), may hold values from -6 to 6
- normalizer: float32 [1024, 32], P('seq', 'head'), may hold values from 3 to 8
- q_index: bfloat16 [1024, 16, 128], P('seq', 'head'), may hold values from -0.5 to 0.5
- k_index: bfloat16 [1024, 128], P('seq'), may hold values from -6 to 6
- index_weight: float32 [1024, 16], P('seq', 'head'), may hold values from -6 to 6
- span_pos: int32 [16], replicated, may hold values from 0 to 15, each once
Outputs:
- grad_query: float32 [1024, 16, 128], P('seq', 'head')
- grad_weight: float32 [1024, 16], P('seq', 'head')
- grad_key: float32 [1024, 128], P('seq')
Inputs may be any that keep to these rules, and one draw needn't show every extreme that they name: `span_pos`: each span position appears exactly once.
All inputs are finite; a program needn't handle non-finite values.
Results may differ from a plain program's by a relative error of at most 0.0085.
Values may be sent and summed in bfloat16 or wider, within the bound.
A program may use at most 64 MiB of HBM per device.

v0:
```python
import jax
import jax.numpy as jnp
from jax import lax
from jax.sharding import PartitionSpec as P

SPAN = 64


softmax_scale = 192.0 ** (-0.5)


def passed_along(x, axis, by):
    devices = lax.axis_size(axis)
    return lax.ppermute(x, axis, [(i, (i + by) % devices) for i in range(devices)])


def key_positions(span_pos, start_row, count):
    row_ids = start_row + jnp.arange(count, dtype=jnp.int32)
    span_index = row_ids // SPAN
    lookup = span_index[:, None] == jnp.arange(span_pos.shape[0], dtype=jnp.int32)[None, :]
    span_base = jnp.sum(jnp.where(lookup, span_pos[None, :], 0), axis=1)
    return span_base * SPAN + row_ids % SPAN


def pass_key_grads(key_accum, key_tile):
    return passed_along(key_accum + key_tile, "seq", 1)


def on_device(q_latent, kv_latent, normalizer, q_index, k_index, index_weight, span_pos):
    q_rows = q_latent.shape[0]
    seq_count = lax.axis_size("seq")
    total_rows = q_rows * seq_count
    my_seq = lax.axis_index("seq")
    query_pos = key_positions(span_pos, my_seq * q_rows, q_rows)
    stored_t = normalizer.T
    weight_t = index_weight.T
    zero_index = jnp.zeros((), jnp.int32)

    def tile_terms(latent_block, index_block, key_start):
        visible = (
            key_positions(span_pos, key_start, latent_block.shape[0])[None, :] <= query_pos[:, None]
        )
        scores = (
            jnp.einsum("qhl,kl->hqk", q_latent, latent_block, preferred_element_type=jnp.float32)
            * softmax_scale
        )
        attention = jnp.where(visible[None], jnp.exp(scores - stored_t[:, :, None]), 0.0)
        index_score = jnp.einsum(
            "qhd,kd->hqk", q_index, index_block, preferred_element_type=jnp.float32
        )
        logit_tile = jnp.sum(weight_t[:, :, None] * jnp.maximum(index_score, 0.0), axis=0)
        return (logit_tile, jnp.sum(attention, axis=0))

    initial = (
        jnp.zeros((q_rows, total_rows), jnp.float32),
        jnp.zeros((q_rows, total_rows), jnp.float32),
    )
    latent_piece = lax.all_gather(kv_latent, "seq", axis=0, tiled=True)
    index_piece = lax.all_gather(k_index, "seq", axis=0, tiled=True)
    piece_rows = latent_piece.shape[0]
    tile_rows = min(piece_rows, q_rows)

    def tile_step(turn_index, state):
        local_off = turn_index * tile_rows
        latent_block = lax.dynamic_slice_in_dim(latent_piece, local_off, tile_rows, 0)
        index_block = lax.dynamic_slice_in_dim(index_piece, local_off, tile_rows, 0)
        logit_tile, target_tile = tile_terms(latent_block, index_block, local_off)
        updated = (
            lax.dynamic_update_slice(state[0], logit_tile, (zero_index, local_off)),
            lax.dynamic_update_slice(state[1], target_tile, (zero_index, local_off)),
        )
        return updated

    folded = lax.fori_loop(0, piece_rows // tile_rows, tile_step, initial)
    logit_part = folded[0]
    target_part = folded[1]
    logit_share = lax.psum_scatter(logit_part, "head", scatter_dimension=1, tiled=True)
    target_share = lax.psum_scatter(
        target_part.astype(jnp.bfloat16), "head", scatter_dimension=1, tiled=True
    ).astype(jnp.float32)
    share_width = logit_share.shape[1]
    visible = (
        key_positions(span_pos, lax.axis_index("head") * share_width, share_width)[None, :]
        <= query_pos[:, None]
    )
    row_peak = lax.pmax(jnp.max(jnp.where(visible, logit_share, -jnp.inf), axis=1), "head")
    expo = jnp.where(visible, jnp.exp(logit_share - row_peak[:, None]), 0.0)
    row_mass, row_norm = lax.psum((jnp.sum(expo, axis=1), jnp.sum(target_share, axis=1)), "head")
    delta_share = (expo / row_mass[:, None] - target_share / row_norm[:, None]).astype(jnp.bfloat16)
    delta = lax.all_gather(delta_share, "head", axis=1, tiled=True)

    def grad_tile(index_block, key_start, grad_query, grad_weight):
        index_score = jnp.einsum(
            "qhd,kd->hqk", q_index, index_block, preferred_element_type=jnp.float32
        )
        delta_tile = lax.dynamic_slice_in_dim(delta, key_start, index_block.shape[0], 1).astype(
            jnp.float32
        )
        grad_weight = grad_weight + jnp.sum(
            delta_tile[None] * jnp.maximum(index_score, 0.0), axis=2
        )
        delta_index = jnp.where(
            index_score > 0, delta_tile[None] * weight_t[:, :, None], 0.0
        ).astype(jnp.bfloat16)
        grad_query = grad_query + jnp.einsum(
            "hqk,kd->qhd", delta_index, index_block, preferred_element_type=jnp.float32
        )
        key_tile = jnp.einsum(
            "hqk,qhd->kd", delta_index, q_index, preferred_element_type=jnp.float32
        )
        return (grad_query, grad_weight, key_tile)

    grad_query0 = jnp.zeros(q_index.shape, jnp.float32)
    grad_weight0 = jnp.zeros(weight_t.shape, jnp.float32)
    key_accum0 = jnp.zeros((q_rows, k_index.shape[1]), jnp.float32)

    def cycle_turn(turn_index, state):
        grad_query, grad_weight, key_accum, index_block = state
        key_start = (my_seq - turn_index) % seq_count * q_rows
        grad_query, grad_weight, key_tile = grad_tile(
            index_block, key_start, grad_query, grad_weight
        )
        key_accum = pass_key_grads(key_accum, key_tile)
        index_block = passed_along(index_block, "seq", 1)
        return (grad_query, grad_weight, key_accum, index_block)

    grad_query, grad_weight, key_accum, _ = lax.fori_loop(
        0, seq_count, cycle_turn, (grad_query0, grad_weight0, key_accum0, k_index)
    )
    grad_key = lax.psum(key_accum, "head")
    return (grad_query, grad_weight.T, grad_key)


def solution(mesh):
    in_specs = (
        P("seq", "head", None),
        P("seq", None),
        P("seq", "head"),
        P("seq", "head", None),
        P("seq", None),
        P("seq", "head"),
        P(),
    )
    out_specs = (P("seq", "head", None), P("seq", "head"), P("seq", None))
    return jax.shard_map(
        on_device, mesh=mesh, in_specs=in_specs, out_specs=out_specs, check_vma=False
    )
```

profile of v0, /device:TPU:0, one launch (start us, length us, event | category | flops | bytes accessed | tf_op | source)
XLA Modules:
  0.0 234.4 jit_solution(7373349838173793865)
XLA Ops:
  7.3 0.8 copy.54
  8.2 0.9 copy.22
  9.1 0.7 select_reduce_fusion.2
  9.9 32.7 %all_gather.9 = bf16[1024,128]{1,0:T(8,128)(2,1)S(1)} all-gather(bf16[128,128]{1,0:T(8,128)(2,1)S(1)} %copy.54), channel_id=1, replica_groups=mesh['seq'=8,'head'=4] {'seq'}, dimensions={0}, use_global_device_ids=true | all-gather | bytes 294912 | tf_op jit(solution)/shard_map/all_gather | solution.py:59
  42.6 11.8 %all-gather.2.cloned.1.call-done = bf16[1024,576]{0,1:T(8,128)(2,1)} async-done(((bf16[128,576]{0,1:T(8,128)(2,1)}), bf16[1024,576]{0,1:T(8,128)(2,1)}) %all-gather.2.cloned.1.call-update) | async-done | bytes 1179664 | tf_op jit(solution)/shard_map/all_gather | solution.py:58
  54.5 14.7 %while.39 = (s32[]{:T(128)}, f32[128,1024]{0,1:T(8,128)S(1)}, bf16[128,1024]{0,1:T(8,128)(2,1)S(1)}, f32[4,128]{1,0:T(4,128)S(1)}, bf16[1024,128]{1,0:T(8,128)(2...) while((s32[]{:T(128)}, f32[128,1024]{0,1:T(8,128)S(1)}, ...), condition=%wide.region_6.7_spmd, body=%wide.region_2.6_spmd.sunk | while | flops 168486528 | bytes 1828627 | solution.py:74
  54.9 1.4 fusion.51
  56.8 1.4 fusion.51
  58.6 1.4 fusion.51
  60.5 1.4 fusion.51
  62.3 1.4 fusion.51
  64.2 1.4 fusion.51
  66.0 1.4 fusion.51
  67.9 1.4 fusion.51
  69.3 0.7 copy-done.2
  70.9 18.2 %reduce-scatter.5.cloned.1.call-done = bf16[128,256]{0,1:T(8,128)(2,1)} async-done(((bf16[128,1024]{0,1:T(8,128)(2,1)}), bf16[128,256]{0,1:T(8,128)(2,1)}) %reduce-scatter.5.cloned.1.call-update) | async-done | bytes 65552 | tf_op jit(solution)/shard_map/reduce_scatter | solution.py:78
  89.1 0.9 convert_reduce_fusion
  90.0 23.3 %reduce-scatter.3.cloned.1.call-done = f32[128,256]{0,1:T(8,128)} async-done(((f32[128,1024]{0,1:T(8,128)}), f32[128,256]{0,1:T(8,128)}) %reduce-scatter.3.cloned.1.call-update) | async-done | bytes 131088 | tf_op jit(solution)/shard_map/reduce_scatter | solution.py:77
  113.3 1.0 fusion.23
  114.3 5.8 %pmax.7 = f32[128]{0:T(128)S(1)} all-reduce(f32[128]{0:T(128)S(1)} %fusion.23), channel_id=1, replica_groups=mesh['seq'=8,'head'=4] {'head'}, use_global_device_ids=true, to_apply=%region_9.10 | all-reduce | flops 128 | bytes 1024 | tf_op jit(solution)/shard_map/pmax | solution.py:86
  120.1 1.0 fusion.24
  121.1 5.7 %all-reduce = (f32[128]{0:T(128)S(1)}, f32[128]{0:T(128)S(1)}) all-reduce(f32[128]{0:T(128)S(1)} %convert_reduce_fusion, f32[128]{0:T(128)S(1)} %fusion.24), channel_id=1, replica_groups=mesh['seq'=8,'head'=4] {'head'}, use_global_device_ids=true, to_apply=%region_14.15 | all-reduce | flops 256 | bytes 2048 | tf_op jit(solution)/shard_map/psum | solution.py:88
  126.8 1.0 fusion.22
  127.8 5.8 %all_gather.11 = bf16[128,1024]{0,1:T(8,128)(2,1)S(1)} all-gather(bf16[128,256]{0,1:T(8,128)(2,1)S(1)} %fusion.22), channel_id=1, replica_groups=mesh['seq'=8,'head'=4] {'head'}, dimensions={1}, use_global_device_ids=true | all-gather | bytes 327680 | tf_op jit(solution)/shard_map/all_gather | solution.py:90
  133.6 62.1 %while.40 = (s32[]{:T(128)}, f32[128,4,128]{2,0,1:T(8,128)S(1)}, f32[4,128]{1,0:T(4,128)S(1)}, f32[128,128]{1,0:T(8,128)S(1)}, bf16[128,128]{1,0:T(8,128)(2,1)S(...) while((s32[]{:T(128)}, f32[128,4,128]{2,0,1:T(8,128)S(1)}, ...), condition=%wide.region_17.18_spmd.clone, body=%wide.region_15.17_spmd.clone.sunk | while | flops 51216912 | bytes 2535827 | solution.py:127
  133.6 1.7 collective-permute-start.1
  135.7 1.5 collective-permute-start
  137.5 2.8 %collective-permute-done.1 = bf16[128,128]{1,0:T(8,128)(2,1)S(1)} collective-permute-done((bf16[128,128]{1,0:T(8,128)(2,1)S(1)}, bf16[128,128]{1,0:T(8,128)(2,1)S(1)}, u32[]{:S(2)}, u32[]{:S(2)}) %collective-permute-start.1) | collective-permute-done | bytes 32800 | tf_op jit(solution)/shard_map/while/body/eval_jaxpr/ppermute | solution.py:14
  140.3 2.5 %collective-permute-done = f32[128,128]{1,0:T(8,128)S(1)} collective-permute-done((f32[128,128]{1,0:T(8,128)S(1)}, f32[128,128]{1,0:T(8,128)S(1)}, u32[]{:S(2)}, u32[]{:S(2)}) %collective-permute-start) | collective-permute-done | bytes 65568 | tf_op jit(solution)/shard_map/while/body/eval_jaxpr/ppermute | solution.py:14
  143.1 1.1 collective-permute-start
  144.6 4.8 %collective-permute-done.1 = bf16[128,128]{1,0:T(8,128)(2,1)S(1)} collective-permute-done((bf16[128,128]{1,0:T(8,128)(2,1)S(1)}, bf16[128,128]{1,0:T(8,128)(2,1)S(1)}, u32[]{:S(2)}, u32[]{:S(2)}) %collective-permute-start.1) | collective-permute-done | bytes 32800 | tf_op jit(solution)/shard_map/while/body/eval_jaxpr/ppermute | solution.py:14
  149.4 0.8 collective-permute-done
  150.9 5.9 %collective-permute-done.1 = bf16[128,128]{1,0:T(8,128)(2,1)S(1)} collective-permute-done((bf16[128,128]{1,0:T(8,128)(2,1)S(1)}, bf16[128,128]{1,0:T(8,128)(2,1)S(1)}, u32[]{:S(2)}, u32[]{:S(2)}) %collective-permute-start.1) | collective-permute-done | bytes 32800 | tf_op jit(solution)/shard_map/while/body/eval_jaxpr/ppermute | solution.py:14
  156.8 0.8 collective-permute-done
  158.3 5.9 %collective-permute-done.1 = bf16[128,128]{1,0:T(8,128)(2,1)S(1)} collective-permute-done((bf16[128,128]{1,0:T(8,128)(2,1)S(1)}, bf16[128,128]{1,0:T(8,128)(2,1)S(1)}, u32[]{:S(2)}, u32[]{:S(2)}) %collective-permute-start.1) | collective-permute-done | bytes 32800 | tf_op jit(solution)/shard_map/while/body/eval_jaxpr/ppermute | solution.py:14
  164.2 0.8 collective-permute-done
  165.8 5.9 %collective-permute-done.1 = bf16[128,128]{1,0:T(8,128)(2,1)S(1)} collective-permute-done((bf16[128,128]{1,0:T(8,128)(2,1)S(1)}, bf16[128,128]{1,0:T(8,128)(2,1)S(1)}, u32[]{:S(2)}, u32[]{:S(2)}) %collective-permute-start.1) | collective-permute-done | bytes 32800 | tf_op jit(solution)/shard_map/while/body/eval_jaxpr/ppermute | solution.py:14
  171.6 1.2 collective-permute-done
  173.6 6.2 %collective-permute-done.1 = bf16[128,128]{1,0:T(8,128)(2,1)S(1)} collective-permute-done((bf16[128,128]{1,0:T(8,128)(2,1)S(1)}, bf16[128,128]{1,0:T(8,128)(2,1)S(1)}, u32[]{:S(2)}, u32[]{:S(2)}) %collective-permute-start.1) | collective-permute-done | bytes 32800 | tf_op jit(solution)/shard_map/while/body/eval_jaxpr/ppermute | solution.py:14
  179.8 1.0 collective-permute-done
  181.6 5.9 %collective-permute-done.1 = bf16[128,128]{1,0:T(8,128)(2,1)S(1)} collective-permute-done((bf16[128,128]{1,0:T(8,128)(2,1)S(1)}, bf16[128,128]{1,0:T(8,128)(2,1)S(1)}, u32[]{:S(2)}, u32[]{:S(2)}) %collective-permute-start.1) | collective-permute-done | bytes 32800 | tf_op jit(solution)/shard_map/while/body/eval_jaxpr/ppermute | solution.py:14
  187.4 0.8 collective-permute-done
  189.0 5.9 %collective-permute-done.1 = bf16[128,128]{1,0:T(8,128)(2,1)S(1)} collective-permute-done((bf16[128,128]{1,0:T(8,128)(2,1)S(1)}, bf16[128,128]{1,0:T(8,128)(2,1)S(1)}, u32[]{:S(2)}, u32[]{:S(2)}) %collective-permute-start.1) | collective-permute-done | bytes 32800 | tf_op jit(solution)/shard_map/while/body/eval_jaxpr/ppermute | solution.py:14
  194.9 0.8 collective-permute-done
  195.7 0.6 copy-done
  196.3 0.9 copy.23
  197.2 29.2 %all-reduce.3.cloned.1.call-done = f32[128,128]{1,0:T(8,128)} async-done(((f32[128,128]{1,0:T(8,128)}), f32[128,128]{1,0:T(8,128)}) %all-reduce.3.cloned.1.call-update) | async-done | bytes 65552 | tf_op jit(solution)/shard_map/psum | solution.py:130
  226.4 1.5 copy.55
  (149 shorter events, 10.1 us)
Async XLA Ops:
  7.2 47.3 %copy-start.6 = (bf16[128,8,576]{0,2,1:T(8,128)(2,1)S(1)}, bf16[128,8,576]{0,2,1:T(8,128)(2,1)}, u32[]{:S(2)}) copy-start(bf16[128,8,576]{0,2,1:T(8,128)(2,1)} %param.11) | copy-start | bytes 3538948
  7.2 47.3 %copy-start.7 = (f32[128,8]{0,1:T(8,128)S(1)}, f32[128,8]{0,1:T(8,128)}, u32[]{:S(2)}) copy-start(f32[128,8]{0,1:T(8,128)} %param.13) | copy-start | bytes 12292
  7.2 47.3 %copy-start.3 = (f32[128,4]{0,1:T(4,128)S(1)}, f32[128,4]{0,1:T(4,128)}, u32[]{:S(2)}) copy-start(f32[128,4]{0,1:T(4,128)} %param.16) | copy-start | bytes 6148
  7.2 47.3 %copy-start.5 = (s32[16]{0:T(128)S(1)}, s32[16]{0:T(128)}, u32[]{:S(2)}) copy-start(s32[16]{0:T(128)} %param.17) | copy-start | bytes 196
  7.2 47.2 %all-gather.2.cloned.1.call-start = ((), (), s32[]{:S(2)}) async-start(), calls=%async_computation.2 | async-start | bytes 1327104 | tf_op jit(solution)/shard_map/all_gather | solution.py:58
  8.1 81.0 %reduce-scatter.5.cloned.1.call-start = ((), (), s32[]{:S(2)}) async-start(), calls=%async_computation.4 | async-start | bytes 327680 | tf_op jit(solution)/shard_map/reduce_scatter | solution.py:78
  69.3 0.7 copy-start.2
  69.3 0.9 copy-start.1
  70.0 43.3 %reduce-scatter.3.cloned.1.call-start = ((), (), s32[]{:S(2)}) async-start(), calls=%async_computation.3 | async-start | bytes 655360 | tf_op jit(solution)/shard_map/reduce_scatter | solution.py:77
  70.7 155.7 %all-reduce.3.cloned.1.call-start = ((), (), s32[]{:S(2)}) async-start(), calls=%async_computation.5 | async-start | bytes 131072 | tf_op jit(solution)/shard_map/psum | solution.py:130
  133.6 6.7 %collective-permute-start.1 = (bf16[128,128]{1,0:T(8,128)(2,1)S(1)}, bf16[128,128]{1,0:T(8,128)(2,1)S(1)}, u32[]{:S(2)}, u32[]{:S(2)}) collective-permute-start(bf16[128,128]{1,0:T(8,128)(2,1)S(1)} %copy.45), channel_id=1, source_target_pairs={{0,4},{4,8},{8,12},{12,16},{16,20},{20,24},{24,28},{28,0},{1,5},{5... | collective-permute-start | bytes 98312 | tf_op jit(solution)/shard_map/while/body/eval_jaxpr/ppermute | solution.py:14
  135.7 7.0 %collective-permute-start = (f32[128,128]{1,0:T(8,128)S(1)}, f32[128,128]{1,0:T(8,128)S(1)}, u32[]{:S(2)}, u32[]{:S(2)}) collective-permute-start(f32[128,128]{1,0:T(8,128)S(1)} %fusion.57), channel_id=1, source_target_pairs={{0,4},{4,8},{8,12},{12,16},{16,20},{20,24},{24,28},{28,0},{1,5},{5... | collective-permute-start | bytes 196616 | tf_op jit(solution)/shard_map/while/body/eval_jaxpr/ppermute | solution.py:14
  142.7 6.6 %collective-permute-start.1 = (bf16[128,128]{1,0:T(8,128)(2,1)S(1)}, bf16[128,128]{1,0:T(8,128)(2,1)S(1)}, u32[]{:S(2)}, u32[]{:S(2)}) collective-permute-start(bf16[128,128]{1,0:T(8,128)(2,1)S(1)} %copy.45), channel_id=1, source_target_pairs={{0,4},{4,8},{8,12},{12,16},{16,20},{20,24},{24,28},{28,0},{1,5},{5... | collective-permute-start | bytes 98312 | tf_op jit(solution)/shard_map/while/body/eval_jaxpr/ppermute | solution.py:14
  143.1 7.0 %collective-permute-start = (f32[128,128]{1,0:T(8,128)S(1)}, f32[128,128]{1,0:T(8,128)S(1)}, u32[]{:S(2)}, u32[]{:S(2)}) collective-permute-start(f32[128,128]{1,0:T(8,128)S(1)} %fusion.57), channel_id=1, source_target_pairs={{0,4},{4,8},{8,12},{12,16},{16,20},{20,24},{24,28},{28,0},{1,5},{5... | collective-permute-start | bytes 196616 | tf_op jit(solution)/shard_map/while/body/eval_jaxpr/ppermute | solution.py:14
  150.2 6.6 %collective-permute-start.1 = (bf16[128,128]{1,0:T(8,128)(2,1)S(1)}, bf16[128,128]{1,0:T(8,128)(2,1)S(1)}, u32[]{:S(2)}, u32[]{:S(2)}) collective-permute-start(bf16[128,128]{1,0:T(8,128)(2,1)S(1)} %copy.45), channel_id=1, source_target_pairs={{0,4},{4,8},{8,12},{12,16},{16,20},{20,24},{24,28},{28,0},{1,5},{5... | collective-permute-start | bytes 98312 | tf_op jit(solution)/shard_map/while/body/eval_jaxpr/ppermute | solution.py:14
  150.6 7.0 %collective-permute-start = (f32[128,128]{1,0:T(8,128)S(1)}, f32[128,128]{1,0:T(8,128)S(1)}, u32[]{:S(2)}, u32[]{:S(2)}) collective-permute-start(f32[128,128]{1,0:T(8,128)S(1)} %fusion.57), channel_id=1, source_target_pairs={{0,4},{4,8},{8,12},{12,16},{16,20},{20,24},{24,28},{28,0},{1,5},{5... | collective-permute-start | bytes 196616 | tf_op jit(solution)/shard_map/while/body/eval_jaxpr/ppermute | solution.py:14
  157.6 6.6 %collective-permute-start.1 = (bf16[128,128]{1,0:T(8,128)(2,1)S(1)}, bf16[128,128]{1,0:T(8,128)(2,1)S(1)}, u32[]{:S(2)}, u32[]{:S(2)}) collective-permute-start(bf16[128,128]{1,0:T(8,128)(2,1)S(1)} %copy.45), channel_id=1, source_target_pairs={{0,4},{4,8},{8,12},{12,16},{16,20},{20,24},{24,28},{28,0},{1,5},{5... | collective-permute-start | bytes 98312 | tf_op jit(solution)/shard_map/while/body/eval_jaxpr/ppermute | solution.py:14
  158.0 7.0 %collective-permute-start = (f32[128,128]{1,0:T(8,128)S(1)}, f32[128,128]{1,0:T(8,128)S(1)}, u32[]{:S(2)}, u32[]{:S(2)}) collective-permute-start(f32[128,128]{1,0:T(8,128)S(1)} %fusion.57), channel_id=1, source_target_pairs={{0,4},{4,8},{8,12},{12,16},{16,20},{20,24},{24,28},{28,0},{1,5},{5... | collective-permute-start | bytes 196616 | tf_op jit(solution)/shard_map/while/body/eval_jaxpr/ppermute | solution.py:14
  165.0 6.6 %collective-permute-start.1 = (bf16[128,128]{1,0:T(8,128)(2,1)S(1)}, bf16[128,128]{1,0:T(8,128)(2,1)S(1)}, u32[]{:S(2)}, u32[]{:S(2)}) collective-permute-start(bf16[128,128]{1,0:T(8,128)(2,1)S(1)} %copy.45), channel_id=1, source_target_pairs={{0,4},{4,8},{8,12},{12,16},{16,20},{20,24},{24,28},{28,0},{1,5},{5... | collective-permute-start | bytes 98312 | tf_op jit(solution)/shard_map/while/body/eval_jaxpr/ppermute | solution.py:14
  165.4 7.4 %collective-permute-start = (f32[128,128]{1,0:T(8,128)S(1)}, f32[128,128]{1,0:T(8,128)S(1)}, u32[]{:S(2)}, u32[]{:S(2)}) collective-permute-start(f32[128,128]{1,0:T(8,128)S(1)} %fusion.57), channel_id=1, source_target_pairs={{0,4},{4,8},{8,12},{12,16},{16,20},{20,24},{24,28},{28,0},{1,5},{5... | collective-permute-start | bytes 196616 | tf_op jit(solution)/shard_map/while/body/eval_jaxpr/ppermute | solution.py:14
  172.8 7.0 %collective-permute-start.1 = (bf16[128,128]{1,0:T(8,128)(2,1)S(1)}, bf16[128,128]{1,0:T(8,128)(2,1)S(1)}, u32[]{:S(2)}, u32[]{:S(2)}) collective-permute-start(bf16[128,128]{1,0:T(8,128)(2,1)S(1)} %copy.45), channel_id=1, source_target_pairs={{0,4},{4,8},{8,12},{12,16},{16,20},{20,24},{24,28},{28,0},{1,5},{5... | collective-permute-start | bytes 98312 | tf_op jit(solution)/shard_map/while/body/eval_jaxpr/ppermute | solution.py:14
  173.2 7.6 %collective-permute-start = (f32[128,128]{1,0:T(8,128)S(1)}, f32[128,128]{1,0:T(8,128)S(1)}, u32[]{:S(2)}, u32[]{:S(2)}) collective-permute-start(f32[128,128]{1,0:T(8,128)S(1)} %fusion.57), channel_id=1, source_target_pairs={{0,4},{4,8},{8,12},{12,16},{16,20},{20,24},{24,28},{28,0},{1,5},{5... | collective-permute-start | bytes 196616 | tf_op jit(solution)/shard_map/while/body/eval_jaxpr/ppermute | solution.py:14
  180.8 6.6 %collective-permute-start.1 = (bf16[128,128]{1,0:T(8,128)(2,1)S(1)}, bf16[128,128]{1,0:T(8,128)(2,1)S(1)}, u32[]{:S(2)}, u32[]{:S(2)}) collective-permute-start(bf16[128,128]{1,0:T(8,128)(2,1)S(1)} %copy.45), channel_id=1, source_target_pairs={{0,4},{4,8},{8,12},{12,16},{16,20},{20,24},{24,28},{28,0},{1,5},{5... | collective-permute-start | bytes 98312 | tf_op jit(solution)/shard_map/while/body/eval_jaxpr/ppermute | solution.py:14
  181.2 7.0 %collective-permute-start = (f32[128,128]{1,0:T(8,128)S(1)}, f32[128,128]{1,0:T(8,128)S(1)}, u32[]{:S(2)}, u32[]{:S(2)}) collective-permute-start(f32[128,128]{1,0:T(8,128)S(1)} %fusion.57), channel_id=1, source_target_pairs={{0,4},{4,8},{8,12},{12,16},{16,20},{20,24},{24,28},{28,0},{1,5},{5... | collective-permute-start | bytes 196616 | tf_op jit(solution)/shard_map/while/body/eval_jaxpr/ppermute | solution.py:14
  188.3 6.6 %collective-permute-start.1 = (bf16[128,128]{1,0:T(8,128)(2,1)S(1)}, bf16[128,128]{1,0:T(8,128)(2,1)S(1)}, u32[]{:S(2)}, u32[]{:S(2)}) collective-permute-start(bf16[128,128]{1,0:T(8,128)(2,1)S(1)} %copy.45), channel_id=1, source_target_pairs={{0,4},{4,8},{8,12},{12,16},{16,20},{20,24},{24,28},{28,0},{1,5},{5... | collective-permute-start | bytes 98312 | tf_op jit(solution)/shard_map/while/body/eval_jaxpr/ppermute | solution.py:14
  188.7 7.0 %collective-permute-start = (f32[128,128]{1,0:T(8,128)S(1)}, f32[128,128]{1,0:T(8,128)S(1)}, u32[]{:S(2)}, u32[]{:S(2)}) collective-permute-start(f32[128,128]{1,0:T(8,128)S(1)} %fusion.57), channel_id=1, source_target_pairs={{0,4},{4,8},{8,12},{12,16},{16,20},{20,24},{24,28},{28,0},{1,5},{5... | collective-permute-start | bytes 196616 | tf_op jit(solution)/shard_map/while/body/eval_jaxpr/ppermute | solution.py:14
  195.7 0.6 copy-start
  195.7 32.2 %copy-start.4 = (f32[4,128]{1,0:T(4,128)}, f32[4,128]{1,0:T(4,128)S(1)}, u32[]{:S(2)}) copy-start(f32[4,128]{1,0:T(4,128)S(1)} %get-tuple-element.497) | copy-start | bytes 6148
Sparse Core Ops, SparseCore 0:
  10.1 44.3 all-gather.1
  70.1 18.9 reduce-scatter.4
  91.6 21.6 reduce-scatter.2
  196.5 29.9 all-reduce.2
where the time goes:
time: 235 us; the launch traced here: 234 us
  waiting for transfers between devices  135 us (57%)
  blocking collectives  49.9 us (21%)
  matrix products  17.5 us (7%)
  between operations  13.9 us (6%)
  other arithmetic  6.6 us (3%)
  local copies, waits for them, and re-layouts  5.83 us (2%)
  starting transfers between devices  4.9 us (2%)
    ppermute x16, waiting for transfers between devices, passed_along(): lax.ppermute(x, axis, [(i, (i + by) % devices) for i in range(devices)])  51.8 us
    all_gather x1, blocking collectives, on_device(): index_piece = lax.all_gather(k_index, 'seq', axis=0, tiled=True)  32.7 us
    psum x1, waiting for transfers between devices, on_device(): grad_key = lax.psum(key_accum, 'head')  29.2 us
    reduce_scatter x1, waiting for transfers between devices, on_device(): lax.psum_scatter(logit_part, 'head', scatter_dimension=1, tiled=True)  23.3 us
    reduce_scatter x1, waiting for transfers between devices, on_device(): lax.psum_scatter(target_part.astype(jnp.bfloat16), 'head', scatter_dimens...  18.2 us
    all_gather x1, waiting for transfers between devices, on_device(): latent_piece = lax.all_gather(kv_latent, 'seq', axis=0, tiled=True)  11.8 us
    dot_general x8, matrix products, tile_terms(): jnp.einsum('qhl,kl->hqk', q_latent, latent_block, preferred_element_type=...  10.9 us
    all_gather x1, blocking collectives, on_device(): delta = lax.all_gather(delta_share, 'head', axis=1, tiled=True)  5.78 us
  transfers between devices with their start and end apart: 20, of which 20 were waited for; matrix products, arithmetic and copies ran while one was open for 4% of the time, Pallas kernels for 0%

commit v1 on v0

v1 whole, which is shorter than its diff:
```python
import functools

import jax
import jax.numpy as jnp
from jax import lax
from jax.experimental import pallas as pl
from jax.experimental.pallas import tpu as pltpu
from jax.sharding import PartitionSpec as P

MESH = pl.DeviceIdType.MESH
F32 = jnp.float32
BF16 = jnp.bfloat16
softmax_scale = 192.0 ** (-0.5)


def kernel(
    n, m, heads, iheads, span,
    q_ref, kv_ref, norm_ref, qi_ref, ki_ref, w_ref, span_ref,
    gq_ref, gw_ref, gk_ref,
    kvbuf, kibuf, normb, wb, attn, wscore, iscore, lbuf, tbuf, l1, t1, l2, t2, lx, tx,
    lall, tall, dbuf, dall, gwacc, gkbuf, gkrecv, hbuf,
    ring_send, ring_recv, core_send, core_recv, s1_send, s1_recv, s2_send, s2_recv,
    d_send, d_recv, gk_send, gk_recv, h_send, h_recv,
):
    s = lax.axis_index("seq")
    h = lax.axis_index("head")
    half = kv_ref.shape[1]
    rows = 2 * half
    c = h % 2
    other = 1 - c
    partner = h + 1 - 2 * c
    near = n // 2

    def seq_at(pos):
        upper = pos // near
        return upper * (2 * (n - 1 - pos) + 1) + (1 - upper) * 2 * pos

    column = s % 2
    place = column * (n - 1 - s // 2) + (1 - column) * (s // 2)

    def seq_off(off):
        return seq_at((place + off + n) % n)

    barrier = pltpu.get_barrier_semaphore()
    for d in range(1, n):
        pl.semaphore_signal(barrier, inc=1, device_id=((s + d) % n, h), device_id_type=MESH)
    for d in range(1, m):
        pl.semaphore_signal(barrier, inc=1, device_id=(s, (h + d) % m), device_id_type=MESH)
    pl.semaphore_wait(barrier, n - 1 + m - 1)

    forward = n // 2
    backward = n - 1 - forward
    offsets = {0: 0}
    for k in range(1, forward + 1):
        offsets[k] = -k
    for k in range(1, backward + 1):
        offsets[forward + k] = k
    order = [0]
    for k in range(1, forward + 1):
        order.append(k)
        if k <= backward:
            order.append(forward + k)

    pending = []

    def remote(src, dst, send, recv, device):
        copy = pltpu.make_async_remote_copy(
            src_ref=src, dst_ref=dst, send_sem=send, recv_sem=recv,
            device_id=device, device_id_type=MESH,
        )
        copy.start()
        pending.append(copy)
        return copy

    def ring_copy(source, target, peer):
        if source == 0:
            kv_src, ki_src = kv_ref.at[c], ki_ref.at[c]
        else:
            kv_src, ki_src = kvbuf.at[source, c], kibuf.at[source, c]
        return (
            remote(kv_src, kvbuf.at[target, c], ring_send.at[target, 0],
                   ring_recv.at[target, 0], (peer, h)),
            remote(ki_src, kibuf.at[target, c], ring_send.at[target, 1],
                   ring_recv.at[target, 1], (peer, h)),
        )

    def core_copy(slot):
        return (
            remote(kvbuf.at[slot, c], kvbuf.at[slot, c], core_send.at[slot, 0],
                   core_recv.at[slot, 0], (s, partner)),
            remote(kibuf.at[slot, c], kibuf.at[slot, c], core_send.at[slot, 1],
                   core_recv.at[slot, 1], (s, partner)),
        )

    following, preceding = seq_off(1), seq_off(-1)
    ring = {1: ring_copy(0, 1, following)}
    if backward:
        ring[forward + 1] = ring_copy(0, forward + 1, preceding)
    kibuf[0] = ki_ref[...]

    for g in range(heads):
        normb[pl.ds(g, rows, stride=heads), :] = jnp.broadcast_to(norm_ref[:, g:g + 1], (rows, rows))
    for g in range(iheads):
        wb[pl.ds(g, rows, stride=iheads), :] = jnp.broadcast_to(w_ref[:, g:g + 1], (rows, rows))

    per_block = rows // span

    def positions(block, index):
        found = jnp.zeros(index.shape, jnp.int32)
        for t in range(per_block):
            base = span_ref[block * per_block + t]
            found = jnp.where(index // span == t, base * span + index % span, found)
        return found

    query_pos = positions(s, lax.broadcasted_iota(jnp.int32, (rows, rows), 0))
    half_pos = positions(s, lax.broadcasted_iota(jnp.int32, (half, rows), 0) + c * half)

    def key_pos(slot, count):
        return positions(seq_off(offsets[slot]), lax.broadcasted_iota(jnp.int32, (count, rows), 1))

    contract_last = (((1,), (1,)), ((), ()))

    def compute(slot):
        kv = (kv_ref[...] if slot == 0 else kvbuf[slot]).reshape(rows, kv_ref.shape[2])
        ki = kibuf[slot].reshape(rows, ki_ref.shape[2])
        scores = lax.dot_general(q_ref[...], kv, contract_last, preferred_element_type=F32)
        attn[...] = jnp.exp(scores * softmax_scale - normb[...])
        rectified = jnp.maximum(
            lax.dot_general(qi_ref[...], ki, contract_last, preferred_element_type=F32), 0.0
        )
        iscore[slot] = rectified
        wscore[...] = wb[...] * rectified
        total = attn[pl.ds(0, rows, stride=heads), :]
        for g in range(1, heads):
            total = total + attn[pl.ds(g, rows, stride=heads), :]
        logit = wscore[pl.ds(0, rows, stride=iheads), :]
        for g in range(1, iheads):
            logit = logit + wscore[pl.ds(g, rows, stride=iheads), :]
        total = jnp.where(key_pos(slot, rows) <= query_pos, total, 0.0).astype(BF16)
        lbuf[slot] = logit.reshape(2, half, rows)
        tbuf[slot] = total.reshape(2, half, rows)
        return (
            remote(lbuf.at[slot, other], l1.at[slot], s1_send.at[slot, 0],
                   s1_recv.at[slot, 0], (s, partner)),
            remote(tbuf.at[slot, other], t1.at[slot], s1_send.at[slot, 1],
                   s1_recv.at[slot, 1], (s, partner)),
        )

    def pair_sum(slot, copies):
        for copy in copies:
            copy.wait_recv()
        l2[slot] = lbuf[slot, c] + l1[slot]
        t2[slot] = (tbuf[slot, c].astype(F32) + t1[slot].astype(F32)).astype(BF16)
        out = []
        for r in range(1, m // 2):
            peer = (h + 2 * r) % m
            out.append(remote(l2.at[slot], lx.at[slot, r - 1], s2_send.at[slot, r - 1, 0],
                              s2_recv.at[slot, r - 1, 0], (s, peer)))
            out.append(remote(t2.at[slot], tx.at[slot, r - 1], s2_send.at[slot, r - 1, 1],
                              s2_recv.at[slot, r - 1, 1], (s, peer)))
        return out

    first = {0: compute(0)}
    second = {}
    last = 0
    for k in range(1, forward + 1):
        arrived = [k] + ([forward + k] if k <= backward else [])
        core = {}
        for slot in arrived:
            for copy in ring[slot]:
                copy.wait_recv()
            if slot <= forward and k < forward:
                ring[slot + 1] = ring_copy(slot, slot + 1, following)
            if slot > forward and k < backward:
                ring[slot + 1] = ring_copy(slot, slot + 1, preceding)
            core[slot] = core_copy(slot)
        for slot in arrived:
            for copy in core[slot]:
                copy.wait_recv()
            first[slot] = compute(slot)
            second[last] = pair_sum(last, first[last])
            last = slot
    second[last] = pair_sum(last, first[last])

    peak = jnp.full((half, 1), -jnp.inf, F32)
    norm = jnp.zeros((half, 1), F32)
    for slot in order:
        for copy in second[slot]:
            copy.wait_recv()
        logit = l2[slot]
        total = t2[slot].astype(F32)
        for r in range(m // 2 - 1):
            logit = logit + lx[slot, r]
            total = total + tx[slot, r].astype(F32)
        logit = jnp.where(key_pos(slot, half) <= half_pos, logit, -jnp.inf)
        lall[slot] = logit
        tall[slot] = total
        peak = jnp.maximum(peak, jnp.max(logit, axis=1, keepdims=True))
        norm = norm + jnp.sum(total, axis=1, keepdims=True)
    mass = jnp.zeros((half, 1), F32)
    for slot in order:
        expo = jnp.exp(lall[slot] - peak)
        lall[slot] = expo
        mass = mass + jnp.sum(expo, axis=1, keepdims=True)
    inv_mass = 1.0 / mass
    inv_norm = 1.0 / norm
    for slot in order:
        dbuf[c, slot] = (lall[slot] * inv_mass - tall[slot] * inv_norm).astype(BF16)
    swap = remote(dbuf.at[c], dbuf.at[c], d_send.at[0], d_recv.at[0], (s, partner))

    token = lax.broadcasted_iota(jnp.int32, (rows * iheads, rows), 0) // iheads
    spread = (token == lax.broadcasted_iota(jnp.int32, (rows * iheads, rows), 1)).astype(F32).astype(BF16)
    gwacc[...] = jnp.zeros_like(gwacc)
    swap.wait_recv()

    incoming = []
    own = None
    for slot in order[::-1]:
        delta = jnp.concatenate([dbuf[0, slot], dbuf[1, slot]], axis=0)
        wide = jnp.dot(spread, delta, preferred_element_type=F32)
        rectified = iscore[slot]
        gwacc[...] += wide * rectified
        part = jnp.where(rectified > 0, wide * wb[...], 0.0).astype(BF16)
        dall[:, slot * rows:(slot + 1) * rows] = part
        grad = lax.dot_general(part, qi_ref[...], (((0,), (0,)), ((), ())), preferred_element_type=F32)
        if slot == 0:
            own = grad
        else:
            gkbuf[slot - 1] = grad.astype(BF16)
            incoming.append((slot, remote(
                gkbuf.at[slot - 1], gkrecv.at[slot - 1], gk_send.at[slot - 1],
                gk_recv.at[slot - 1], (seq_off(offsets[slot]), h))))

    keys = kibuf[...].reshape(n * rows, ki_ref.shape[2])
    gq_ref[...] = jnp.dot(dall[...], keys, preferred_element_type=F32)
    wscore[...] = jnp.broadcast_to(jnp.sum(gwacc[...], axis=1, keepdims=True), wscore.shape)
    for g in range(iheads):
        gw_ref[:, g:g + 1] = wscore[pl.ds(g, rows, stride=iheads), :][:, 0:1]

    for slot, copy in incoming:
        copy.wait_recv()
        own = own + gkrecv[slot - 1].astype(F32)
    hbuf[h] = own.astype(BF16)
    swaps = []
    for r in range(1, m):
        peer = (h + r) % m
        swaps.append(remote(hbuf.at[h], hbuf.at[h], h_send.at[r - 1], h_recv.at[r - 1], (s, peer)))
    for copy in swaps:
        copy.wait_recv()
    result = hbuf[0].astype(F32)
    for r in range(1, m):
        result = result + hbuf[r].astype(F32)
    gk_ref[...] = result
    for copy in pending:
        copy.wait_send()


def solution(mesh):
    n, m = mesh.shape["seq"], mesh.shape["head"]

    def on_device(q_latent, kv_latent, normalizer, q_index, k_index, index_weight, span_pos):
        rows, heads, latent = q_latent.shape
        iheads, idim = q_index.shape[1:]
        half = rows // 2
        span = rows * n // span_pos.shape[0]
        peers = max(m // 2 - 1, 1)
        V = pltpu.VMEM
        D = pltpu.SemaphoreType.DMA
        scratch = [
            V((n, 2, half, latent), BF16), V((n, 2, half, idim), BF16),
            V((rows * heads, rows), F32), V((rows * iheads, rows), F32),
            V((rows * heads, rows), F32), V((rows * iheads, rows), F32),
            V((n, rows * iheads, rows), F32),
            V((n, 2, half, rows), F32), V((n, 2, half, rows), BF16),
            V((n, half, rows), F32), V((n, half, rows), BF16),
            V((n, half, rows), F32), V((n, half, rows), BF16),
            V((n, peers, half, rows), F32), V((n, peers, half, rows), BF16),
            V((n, half, rows), F32), V((n, half, rows), F32),
            V((2, n, half, rows), BF16), V((rows * iheads, n * rows), BF16),
            V((rows * iheads, rows), F32),
            V((n - 1, rows, idim), BF16), V((n - 1, rows, idim), BF16),
            V((m, rows, idim), BF16),
            D((n, 2)), D((n, 2)), D((n, 2)), D((n, 2)), D((n, 2)), D((n, 2)),
            D((n, peers, 2)), D((n, peers, 2)), D((1,)), D((1,)),
            D((n - 1,)), D((n - 1,)), D((m - 1,)), D((m - 1,)),
        ]
        vmem = pl.BlockSpec(memory_space=pltpu.VMEM)
        gq, gw, gk = pl.pallas_call(
            functools.partial(kernel, n, m, heads, iheads, span),
            out_shape=(
                jax.ShapeDtypeStruct((rows * iheads, idim), F32),
                jax.ShapeDtypeStruct((rows, iheads), F32),
                jax.ShapeDtypeStruct((rows, idim), F32),
            ),
            in_specs=[vmem] * 6 + [pl.BlockSpec(memory_space=pltpu.SMEM)],
            out_specs=(vmem, vmem, vmem),
            scratch_shapes=scratch,
            compiler_params=pltpu.CompilerParams(
                collective_id=0, has_side_effects=True, vmem_limit_bytes=60 * 2 ** 20
            ),
        )(
            q_latent.reshape(rows * heads, latent), kv_latent.reshape(2, half, latent),
            normalizer, q_index.reshape(rows * iheads, idim),
            k_index.reshape(2, half, idim), index_weight, span_pos,
        )
        return gq.reshape(rows, iheads, idim), gw, gk

    in_specs = (
        P("seq", "head", None), P("seq", None), P("seq", "head"), P("seq", "head", None),
        P("seq", None), P("seq", "head"), P(),
    )
    out_specs = (P("seq", "head", None), P("seq", "head"), P("seq", None))
    return jax.shard_map(
        on_device, mesh=mesh, in_specs=in_specs, out_specs=out_specs, check_vma=False
    )
```

time: 235 us -> 54.4 us (0.23)
  waiting for transfers between devices: 135 us -> 0 us
  blocking collectives: 49.9 us -> 0 us
  Pallas kernels: 0 us -> 41.3 us
  matrix products: 17.5 us -> 0 us
  between operations: 13.9 us -> 0.64 us
  other arithmetic: 6.6 us -> 0 us
  local copies, waits for them, and re-layouts: 5.83 us -> 12 us
  starting transfers between devices: 4.9 us -> 0 us
    ppermute x16 -> x0, waiting for transfers between devices: 51.8 us -> none  [passed_along(): lax.ppermute(x, axis, [(i, (i + by) % devices) for i in range(devices)])]
    reduce_scatter x2 -> x0, waiting for transfers between devices: 41.5 us -> none  [the longest x1 23.3 us: on_device(): lax.psum_scatter(logit_part, 'head', scatter_dimension=1, tiled=True)]
    pallas_call x0 -> x1, Pallas kernels: none -> 41.3 us  [on_device(): pl.pallas_call(functools.partial(kernel, n, m, heads, iheads, span), out_...]
    all_gather x2 -> x0, blocking collectives: 38.5 us -> none  [the longest x1 32.7 us: on_device(): index_piece = lax.all_gather(k_index, 'seq', axis=0, tiled=True)]
    psum x1 -> x0, waiting for transfers between devices: 29.2 us -> none  [on_device(): grad_key = lax.psum(key_accum, 'head')]
    dot_general x40 -> x0, matrix products: 17.5 us -> none  [the longest x8 10.9 us: tile_terms(): jnp.einsum('qhl,kl->hqk', q_latent, latent_block, preferred_element_type=...]
    all_gather x1 -> x0, waiting for transfers between devices: 11.8 us -> none  [on_device(): latent_piece = lax.all_gather(kv_latent, 'seq', axis=0, tiled=True)]
    unnamed x20 -> x7, local copies, waits for them, and re-layouts: 5.55 us -> 12 us
  transfers between devices with their start and end apart: 20 -> 0, of which waited for: 20 -> 0; matrix products, arithmetic and copies ran while one was open for 4% -> 0% of each run, Pallas kernels for 0% -> 0%
where the time goes in v1:
time: 54.4 us; the launch traced here: 54 us
  Pallas kernels  41.3 us (76%)
  local copies, waits for them, and re-layouts  12 us (22%)
  between operations  0.64 us (1%)
    pallas_call x1, Pallas kernels, on_device(): pl.pallas_call(functools.partial(kernel, n, m, heads, iheads, span), out_...  41.3 us
    unnamed x7, local copies, waits for them, and re-layouts  12 us

profile of v1, /device:TPU:0, one launch (start us, length us, event | category | flops | bytes accessed | tf_op | source)
XLA Modules:
  0.0 54.0 jit_solution(6456349107246395396)
XLA Ops:
  0.6 1.4 %copy.12.norm_ref = f32[128,8]{1,0:T(8,128)} copy(f32[128,8]{0,1:T(8,128)} %param.9) | data formatting | bytes 8192 | tf_op args[2]
  2.0 1.4 %copy.13.w_ref = f32[128,4]{1,0:T(8,128)} copy(f32[128,4]{0,1:T(4,128)} %param.12) | data formatting | bytes 4096 | tf_op args[5]
  3.5 1.7 %copy.11 = bf16[128,576]{1,0:T(8,128)(2,1)} copy(bf16[128,576]{0,1:T(8,128)(2,1)} %param.8) | data formatting | bytes 294912 | tf_op args[1]
  5.2 2.9 %copy.10 = bf16[128,8,576]{2,1,0:T(8,128)(2,1)} copy(bf16[128,8,576]{0,2,1:T(8,128)(2,1)} %param.7) | data formatting | bytes 2359296 | tf_op args[0]
  8.0 41.3 %shard_map.94 = (f32[512,128]{1,0:T(8,128)}, f32[128,4]{1,0:T(8,128)}, f32[128,128]{1,0:T(8,128)}) custom-call(bf16[1024,576]{1,0:T(8,128)(2,1)} %bitcast.5, bf16[2,64,576]{2,1,0:T(8,128)(2,1)} %bitcast.6, f32[128,8]{1,0:T(8,128)} %copy.12.norm_ref, bf16[512,128]{1,0:T(8,128)(2,1)} %bitcast.8, bf16[2,64,128]{2,1,0:T(8,128)(2,1)} %bitcast.9, ...), custom_call_target="tpu_custom_call" | custom-call | tf_op jit(solution)/shard_map/pallas_call | solution.py:288
  49.4 1.5 %copy.14 = f32[128,4]{0,1:T(4,128)} copy(f32[128,4]{1,0:T(8,128)} %get-tuple-element.10) | data formatting | bytes 4096
  50.9 1.7 %copy.17 = f32[128,4,128]{2,1,0:T(4,128)} copy(f32[128,4,128]{2,1,0:T(4,128)} %bitcast.7) | data formatting | bytes 524288
  52.5 1.5 %copy.18 = f32[128,128]{1,0:T(8,128)} copy(f32[128,128]{1,0:T(8,128)} %get-tuple-element.17) | data formatting | bytes 131072

commit v2 on v1

--- a/solution.py
+++ b/solution.py
@@ -17,15 +17,16 @@
     n, m, heads, iheads, span,
     q_ref, kv_ref, norm_ref, qi_ref, ki_ref, w_ref, span_ref,
     gq_ref, gw_ref, gk_ref,
-    kvbuf, kibuf, normb, wb, attn, wscore, iscore, lbuf, tbuf, l1, t1, l2, t2, lx, tx,
+    kvbuf, kibuf, qraw, qrows, normb, wb, attn, wscore, iscore, lbuf, tbuf, l1, t1, l2, t2, lx, tx,
     lall, tall, dbuf, dall, gwacc, gkbuf, gkrecv, hbuf,
-    ring_send, ring_recv, core_send, core_recv, s1_send, s1_recv, s2_send, s2_recv,
+    q_sem, ring_send, ring_recv, core_send, core_recv, s1_send, s1_recv, s2_send, s2_recv,
     d_send, d_recv, gk_send, gk_recv, h_send, h_recv,
 ):
     s = lax.axis_index("seq")
     h = lax.axis_index("head")
-    half = kv_ref.shape[1]
-    rows = 2 * half
+    rows = kv_ref.shape[2]
+    half = rows // 2
+    latent = 2 * kv_ref.shape[1]
     c = h % 2
     other = 1 - c
     partner = h + 1 - 2 * c
@@ -41,6 +42,9 @@
     def seq_off(off):
         return seq_at((place + off + n) % n)
 
+    loads = [pltpu.make_async_copy(q_ref.at[g], qraw.at[g], q_sem.at[g]) for g in range(heads)]
+    for load in loads:
+        load.start()
     barrier = pltpu.get_barrier_semaphore()
     for d in range(1, n):
         pl.semaphore_signal(barrier, inc=1, device_id=((s + d) % n, h), device_id_type=MESH)
@@ -99,9 +103,12 @@
     kibuf[0] = ki_ref[...]
 
     for g in range(heads):
-        normb[pl.ds(g, rows, stride=heads), :] = jnp.broadcast_to(norm_ref[:, g:g + 1], (rows, rows))
+        normb[g * rows:(g + 1) * rows, :] = jnp.broadcast_to(norm_ref[g:g + 1, :], (rows, rows)).T
     for g in range(iheads):
-        wb[pl.ds(g, rows, stride=iheads), :] = jnp.broadcast_to(w_ref[:, g:g + 1], (rows, rows))
+        wb[pl.ds(g, rows, stride=iheads), :] = jnp.broadcast_to(w_ref[g:g + 1, :], (rows, rows)).T
+    for g, load in enumerate(loads):
+        load.wait()
+        qrows[g * rows:(g + 1) * rows, :] = qraw[g].T
 
     per_block = rows // span
 
@@ -120,31 +127,38 @@
 
     contract_last = (((1,), (1,)), ((), ()))
 
-    def compute(slot):
-        kv = (kv_ref[...] if slot == 0 else kvbuf[slot]).reshape(rows, kv_ref.shape[2])
-        ki = kibuf[slot].reshape(rows, ki_ref.shape[2])
-        scores = lax.dot_general(q_ref[...], kv, contract_last, preferred_element_type=F32)
-        attn[...] = jnp.exp(scores * softmax_scale - normb[...])
-        rectified = jnp.maximum(
-            lax.dot_general(qi_ref[...], ki, contract_last, preferred_element_type=F32), 0.0
-        )
-        iscore[slot] = rectified
-        wscore[...] = wb[...] * rectified
-        total = attn[pl.ds(0, rows, stride=heads), :]
-        for g in range(1, heads):
-            total = total + attn[pl.ds(g, rows, stride=heads), :]
-        logit = wscore[pl.ds(0, rows, stride=iheads), :]
-        for g in range(1, iheads):
-            logit = logit + wscore[pl.ds(g, rows, stride=iheads), :]
-        total = jnp.where(key_pos(slot, rows) <= query_pos, total, 0.0).astype(BF16)
-        lbuf[slot] = logit.reshape(2, half, rows)
-        tbuf[slot] = total.reshape(2, half, rows)
-        return (
-            remote(lbuf.at[slot, other], l1.at[slot], s1_send.at[slot, 0],
-                   s1_recv.at[slot, 0], (s, partner)),
-            remote(tbuf.at[slot, other], t1.at[slot], s1_send.at[slot, 1],
-                   s1_recv.at[slot, 1], (s, partner)),
-        )
+    def compute(slots):
+        width = len(slots) * rows
+        kv = jnp.concatenate(
+            [(kv_ref[...] if slot == 0 else kvbuf[slot]).reshape(latent, rows) for slot in slots], axis=1
+        )
+        scores = jnp.dot(qrows[...], kv, preferred_element_type=F32)
+        attn[:, 0:width] = scores
+        keys = jnp.concatenate([kibuf[slot].reshape(rows, ki_ref.shape[2]) for slot in slots], axis=0)
+        raw_index = lax.dot_general(qi_ref[...], keys, contract_last, preferred_element_type=F32)
+        out = {}
+        for i, slot in enumerate(slots):
+            lanes = slice(i * rows, (i + 1) * rows)
+            rectified = jnp.maximum(raw_index[:, lanes], 0.0)
+            iscore[slot] = rectified
+            wscore[...] = wb[...] * rectified
+            logit = wscore[pl.ds(0, rows, stride=iheads), :]
+            for g in range(1, iheads):
+                logit = logit + wscore[pl.ds(g, rows, stride=iheads), :]
+            lbuf[slot] = logit.reshape(2, half, rows)
+            total = jnp.zeros((rows, rows), F32)
+            for g in range(heads):
+                band = slice(g * rows, (g + 1) * rows)
+                total = total + jnp.exp(attn[band, lanes] * softmax_scale - normb[band, :])
+            total = jnp.where(key_pos(slot, rows) <= query_pos, total, 0.0).astype(BF16)
+            tbuf[slot] = total.reshape(2, half, rows)
+            out[slot] = (
+                remote(lbuf.at[slot, other], l1.at[slot], s1_send.at[slot, 0],
+                       s1_recv.at[slot, 0], (s, partner)),
+                remote(tbuf.at[slot, other], t1.at[slot], s1_send.at[slot, 1],
+                       s1_recv.at[slot, 1], (s, partner)),
+            )
+        return out
 
     def pair_sum(slot, copies):
         for copy in copies:
@@ -160,9 +174,9 @@
                               s2_recv.at[slot, r - 1, 1], (s, peer)))
         return out
 
-    first = {0: compute(0)}
+    first = compute([0])
     second = {}
-    last = 0
+    waiting = [0]
     for k in range(1, forward + 1):
         arrived = [k] + ([forward + k] if k <= backward else [])
         core = {}
@@ -174,13 +188,15 @@
             if slot > forward and k < backward:
                 ring[slot + 1] = ring_copy(slot, slot + 1, preceding)
             core[slot] = core_copy(slot)
+        for slot in waiting:
+            second[slot] = pair_sum(slot, first[slot])
         for slot in arrived:
             for copy in core[slot]:
                 copy.wait_recv()
-            first[slot] = compute(slot)
-            second[last] = pair_sum(last, first[last])
-            last = slot
-    second[last] = pair_sum(last, first[last])
+        first.update(compute(arrived))
+        waiting = arrived
+    for slot in waiting:
+        second[slot] = pair_sum(slot, first[slot])
 
     peak = jnp.full((half, 1), -jnp.inf, F32)
     norm = jnp.zeros((half, 1), F32)
@@ -233,9 +249,8 @@
 
     keys = kibuf[...].reshape(n * rows, ki_ref.shape[2])
     gq_ref[...] = jnp.dot(dall[...], keys, preferred_element_type=F32)
-    wscore[...] = jnp.broadcast_to(jnp.sum(gwacc[...], axis=1, keepdims=True), wscore.shape)
     for g in range(iheads):
-        gw_ref[:, g:g + 1] = wscore[pl.ds(g, rows, stride=iheads), :][:, 0:1]
+        gw_ref[g:g + 1, :] = jnp.sum(gwacc[pl.ds(g, rows, stride=iheads), :].T, axis=0, keepdims=True)
 
     for slot, copy in incoming:
         copy.wait_recv()
@@ -267,9 +282,10 @@
         V = pltpu.VMEM
         D = pltpu.SemaphoreType.DMA
         scratch = [
-            V((n, 2, half, latent), BF16), V((n, 2, half, idim), BF16),
+            V((n, 2, latent // 2, rows), BF16), V((n, 2, half, idim), BF16),
+            V((heads, latent, rows), BF16), V((rows * heads, latent), BF16),
             V((rows * heads, rows), F32), V((rows * iheads, rows), F32),
-            V((rows * heads, rows), F32), V((rows * iheads, rows), F32),
+            V((rows * heads, 2 * rows), F32), V((rows * iheads, rows), F32),
             V((n, rows * iheads, rows), F32),
             V((n, 2, half, rows), F32), V((n, 2, half, rows), BF16),
             V((n, half, rows), F32), V((n, half, rows), BF16),
@@ -280,7 +296,7 @@
             V((rows * iheads, rows), F32),
             V((n - 1, rows, idim), BF16), V((n - 1, rows, idim), BF16),
             V((m, rows, idim), BF16),
-            D((n, 2)), D((n, 2)), D((n, 2)), D((n, 2)), D((n, 2)), D((n, 2)),
+            D((heads,)), D((n, 2)), D((n, 2)), D((n, 2)), D((n, 2)), D((n, 2)), D((n, 2)),
             D((n, peers, 2)), D((n, peers, 2)), D((1,)), D((1,)),
             D((n - 1,)), D((n - 1,)), D((m - 1,)), D((m - 1,)),
         ]
@@ -289,21 +305,21 @@
             functools.partial(kernel, n, m, heads, iheads, span),
             out_shape=(
                 jax.ShapeDtypeStruct((rows * iheads, idim), F32),
-                jax.ShapeDtypeStruct((rows, iheads), F32),
+                jax.ShapeDtypeStruct((iheads, rows), F32),
                 jax.ShapeDtypeStruct((rows, idim), F32),
             ),
-            in_specs=[vmem] * 6 + [pl.BlockSpec(memory_space=pltpu.SMEM)],
+            in_specs=[pl.BlockSpec(memory_space=pl.ANY)] + [vmem] * 5 + [pl.BlockSpec(memory_space=pltpu.SMEM)],
             out_specs=(vmem, vmem, vmem),
             scratch_shapes=scratch,
             compiler_params=pltpu.CompilerParams(
                 collective_id=0, has_side_effects=True, vmem_limit_bytes=60 * 2 ** 20
             ),
         )(
-            q_latent.reshape(rows * heads, latent), kv_latent.reshape(2, half, latent),
-            normalizer, q_index.reshape(rows * iheads, idim),
-            k_index.reshape(2, half, idim), index_weight, span_pos,
-        )
-        return gq.reshape(rows, iheads, idim), gw, gk
+            q_latent.transpose(1, 2, 0), kv_latent.T.reshape(2, latent // 2, rows),
+            normalizer.T, q_index.reshape(rows * iheads, idim),
+            k_index.reshape(2, half, idim), index_weight.T, span_pos,
+        )
+        return gq.reshape(rows, iheads, idim), gw.T, gk
 
     in_specs = (
         P("seq", "head", None), P("seq", None), P("seq", "head"), P("seq", "head", None),

time: 54.4 us -> 45.6 us (0.84)
  local copies, waits for them, and re-layouts: 12 us -> 4.4 us
  Pallas kernels: 41.3 us -> 40.3 us
    unnamed x7 -> x3, local copies, waits for them, and re-layouts: 12 us -> 4.4 us
    pallas_call x1, Pallas kernels: 41.3 us -> 40.3 us  [on_device(): pl.pallas_call(functools.partial(kernel, n, m, heads, iheads, span), out_...]
where the time goes in v2:
time: 45.6 us; the launch traced here: 45.3 us
  Pallas kernels  40.3 us (88%)
  local copies, waits for them, and re-layouts  4.4 us (10%)
  between operations  0.64 us (1%)
    pallas_call x1, Pallas kernels, on_device(): pl.pallas_call(functools.partial(kernel, n, m, heads, iheads, span), out_...  40.3 us
    unnamed x3, local copies, waits for them, and re-layouts  4.4 us

profile of v2, /device:TPU:0, one launch (start us, length us, event | category | flops | bytes accessed | tf_op | source)
XLA Modules:
  0.0 45.3 jit_solution(17059239076198869571)
XLA Ops:
  0.6 40.3 %shard_map.94 = (f32[512,128]{1,0:T(8,128)}, f32[4,128]{1,0:T(4,128)}, f32[128,128]{1,0:T(8,128)}) custom-call(bf16[8,576,128]{2,1,0:T(8,128)(2,1)} %bitcast.10, bf16[2,288,128]{2,1,0:T(8,128)(2,1)} %bitcast.12, f32[8,128]{1,0:T(8,128)} %bitcast.15, bf16[512,128]{1,0:T(8,128)(2,1)} %bitcast.13, bf16[2,64,128]{2,1,0:T(8,128)(2,1)} %bitcast.14, ...), custom_call_target="tpu_custom_call" | custom-call | tf_op jit(solution)/shard_map/pallas_call | solution.py:304
  40.9 1.7 %copy.13 = f32[128,4,128]{2,1,0:T(4,128)} copy(f32[128,4,128]{2,1,0:T(4,128)} %bitcast.11) | data formatting | bytes 524288
  42.6 1.3 %copy.14 = f32[128,4]{0,1:T(4,128)} copy(f32[128,4]{0,1:T(4,128)} %bitcast.17) | data formatting | bytes 4096
  43.9 1.5 %copy.15 = f32[128,128]{1,0:T(8,128)} copy(f32[128,128]{1,0:T(8,128)} %get-tuple-element.14) | data formatting | bytes 131072

commit v3 on v2

--- a/solution.py
+++ b/solution.py
@@ -14,7 +14,7 @@
 
 
 def kernel(
-    n, m, heads, iheads, span,
+    n, m, heads, iheads, span, pieces,
     q_ref, kv_ref, norm_ref, qi_ref, ki_ref, w_ref, span_ref,
     gq_ref, gw_ref, gk_ref,
     kvbuf, kibuf, qraw, qrows, normb, wb, attn, wscore, iscore, lbuf, tbuf, l1, t1, l2, t2, lx, tx,
@@ -27,6 +27,7 @@
     rows = kv_ref.shape[2]
     half = rows // 2
     latent = 2 * kv_ref.shape[1]
+    depth = kv_ref.shape[1] // pieces
     c = h % 2
     other = 1 - c
     partner = h + 1 - 2 * c
@@ -76,30 +77,29 @@
         pending.append(copy)
         return copy
 
-    def ring_copy(source, target, peer):
+    def view(kv, ki, piece):
+        if piece == pieces:
+            return ki
+        return kv.at[pl.ds(piece * depth, depth)]
+
+    def ring_copy(source, target, peer, piece):
         if source == 0:
-            kv_src, ki_src = kv_ref.at[c], ki_ref.at[c]
+            src = view(kv_ref.at[c], ki_ref.at[c], piece)
         else:
-            kv_src, ki_src = kvbuf.at[source, c], kibuf.at[source, c]
-        return (
-            remote(kv_src, kvbuf.at[target, c], ring_send.at[target, 0],
-                   ring_recv.at[target, 0], (peer, h)),
-            remote(ki_src, kibuf.at[target, c], ring_send.at[target, 1],
-                   ring_recv.at[target, 1], (peer, h)),
-        )
-
-    def core_copy(slot):
-        return (
-            remote(kvbuf.at[slot, c], kvbuf.at[slot, c], core_send.at[slot, 0],
-                   core_recv.at[slot, 0], (s, partner)),
-            remote(kibuf.at[slot, c], kibuf.at[slot, c], core_send.at[slot, 1],
-                   core_recv.at[slot, 1], (s, partner)),
-        )
+            src = view(kvbuf.at[source, c], kibuf.at[source, c], piece)
+        return remote(src, view(kvbuf.at[target, c], kibuf.at[target, c], piece),
+                      ring_send.at[target, piece], ring_recv.at[target, piece], (peer, h))
+
+    def core_copy(slot, piece):
+        block = view(kvbuf.at[slot, c], kibuf.at[slot, c], piece)
+        return remote(block, block, core_send.at[slot, piece], core_recv.at[slot, piece], (s, partner))
 
     following, preceding = seq_off(1), seq_off(-1)
-    ring = {1: ring_copy(0, 1, following)}
-    if backward:
-        ring[forward + 1] = ring_copy(0, forward + 1, preceding)
+    ring = {}
+    for piece in range(pieces + 1):
+        ring[1, piece] = ring_copy(0, 1, following, piece)
+        if backward:
+            ring[forward + 1, piece] = ring_copy(0, forward + 1, preceding, piece)
     kibuf[0] = ki_ref[...]
 
     for g in range(heads):
@@ -180,19 +180,19 @@
     for k in range(1, forward + 1):
         arrived = [k] + ([forward + k] if k <= backward else [])
         core = {}
-        for slot in arrived:
-            for copy in ring[slot]:
-                copy.wait_recv()
-            if slot <= forward and k < forward:
-                ring[slot + 1] = ring_copy(slot, slot + 1, following)
-            if slot > forward and k < backward:
-                ring[slot + 1] = ring_copy(slot, slot + 1, preceding)
-            core[slot] = core_copy(slot)
+        for piece in range(pieces + 1):
+            for slot in arrived:
+                ring[slot, piece].wait_recv()
+                if slot <= forward and k < forward:
+                    ring[slot + 1, piece] = ring_copy(slot, slot + 1, following, piece)
+                if slot > forward and k < backward:
+                    ring[slot + 1, piece] = ring_copy(slot, slot + 1, preceding, piece)
+                core[slot, piece] = core_copy(slot, piece)
         for slot in waiting:
             second[slot] = pair_sum(slot, first[slot])
         for slot in arrived:
-            for copy in core[slot]:
-                copy.wait_recv()
+            for piece in range(pieces + 1):
+                core[slot, piece].wait_recv()
         first.update(compute(arrived))
         waiting = arrived
     for slot in waiting:
@@ -270,6 +270,12 @@
         copy.wait_send()
 
 
+def write_out(gq_in, gw_in, gk_in, gq_ref, gw_ref, gk_ref):
+    gq_ref[...] = gq_in[...]
+    gw_ref[...] = gw_in[...]
+    gk_ref[...] = gk_in[...]
+
+
 def solution(mesh):
     n, m = mesh.shape["seq"], mesh.shape["head"]
 
@@ -278,6 +284,7 @@
         iheads, idim = q_index.shape[1:]
         half = rows // 2
         span = rows * n // span_pos.shape[0]
+        pieces = 3 if latent % 96 == 0 else 1
         peers = max(m // 2 - 1, 1)
         V = pltpu.VMEM
         D = pltpu.SemaphoreType.DMA
@@ -296,13 +303,14 @@
             V((rows * iheads, rows), F32),
             V((n - 1, rows, idim), BF16), V((n - 1, rows, idim), BF16),
             V((m, rows, idim), BF16),
-            D((heads,)), D((n, 2)), D((n, 2)), D((n, 2)), D((n, 2)), D((n, 2)), D((n, 2)),
+            D((heads,)), D((n, pieces + 1)), D((n, pieces + 1)), D((n, pieces + 1)),
+            D((n, pieces + 1)), D((n, 2)), D((n, 2)),
             D((n, peers, 2)), D((n, peers, 2)), D((1,)), D((1,)),
             D((n - 1,)), D((n - 1,)), D((m - 1,)), D((m - 1,)),
         ]
         vmem = pl.BlockSpec(memory_space=pltpu.VMEM)
-        gq, gw, gk = pl.pallas_call(
-            functools.partial(kernel, n, m, heads, iheads, span),
+        results = pl.pallas_call(
+            functools.partial(kernel, n, m, heads, iheads, span, pieces),
             out_shape=(
                 jax.ShapeDtypeStruct((rows * iheads, idim), F32),
                 jax.ShapeDtypeStruct((iheads, rows), F32),
@@ -319,6 +327,12 @@
             normalizer.T, q_index.reshape(rows * iheads, idim),
             k_index.reshape(2, half, idim), index_weight.T, span_pos,
         )
+        gq, gw, gk = pl.pallas_call(
+            write_out,
+            out_shape=tuple(jax.ShapeDtypeStruct(x.shape, x.dtype) for x in results),
+            in_specs=[vmem] * 3,
+            out_specs=(vmem,) * 3,
+        )(*results)
         return gq.reshape(rows, iheads, idim), gw.T, gk
 
     in_specs = (

time: 45.6 us -> 42.1 us (0.923)
  local copies, waits for them, and re-layouts: 4.4 us -> 0 us
  Pallas kernels: 40.3 us -> 41.3 us
    unnamed x3 -> x0, local copies, waits for them, and re-layouts: 4.4 us -> none
    pallas_call x1 -> x2, Pallas kernels: 40.3 us -> 41.3 us  [the longest x1 39.6 us: on_device(): pl.pallas_call(functools.partial(kernel, n, m, heads, iheads, span, piece...]
where the time goes in v3:
time: 42.1 us; the launch traced here: 41.9 us
  Pallas kernels  41.3 us (98%)
  between operations  0.64 us (2%)
    pallas_call x1, Pallas kernels, on_device(): pl.pallas_call(functools.partial(kernel, n, m, heads, iheads, span, piece...  39.6 us
    pallas_call x1, Pallas kernels, on_device(): pl.pallas_call(write_out, out_shape=tuple((jax.ShapeDtypeStruct(x.shape,...  1.69 us

profile of v3, /device:TPU:0, one launch (start us, length us, event | category | flops | bytes accessed | tf_op | source)
XLA Modules:
  0.0 41.9 jit_solution(4303323381789781761)
XLA Ops:
  0.6 39.6 %shard_map.94 = (f32[512,128]{1,0:T(8,128)}, f32[4,128]{1,0:T(4,128)}, f32[128,128]{1,0:T(8,128)}) custom-call(bf16[8,576,128]{2,1,0:T(8,128)(2,1)} %bitcast.10, bf16[2,288,128]{2,1,0:T(8,128)(2,1)} %bitcast.11, f32[8,128]{1,0:T(8,128)} %bitcast.14, bf16[512,128]{1,0:T(8,128)(2,1)} %bitcast.12, bf16[2,64,128]{2,1,0:T(8,128)(2,1)} %bitcast.13, ...), custom_call_target="tpu_custom_call" | custom-call | tf_op jit(solution)/shard_map/pallas_call | solution.py:312
  40.2 1.7 %shard_map.95 = (f32[512,128]{1,0:T(8,128)}, f32[4,128]{1,0:T(4,128)}, f32[128,128]{1,0:T(8,128)}) custom-call(f32[512,128]{1,0:T(8,128)} %get-tuple-element.9.gq_in, f32[4,128]{1,0:T(4,128)} %get-tuple-element.10.gw_in, f32[128,128]{1,0:T(8,128)} %get-tuple-element.11.gk_in), custom_call_target="tpu_custom_call" | custom-call | tf_op jit(solution)/shard_map/pallas_call | solution.py:330

commit v4 on v3

--- a/solution.py
+++ b/solution.py
@@ -18,9 +18,9 @@
     q_ref, kv_ref, norm_ref, qi_ref, ki_ref, w_ref, span_ref,
     gq_ref, gw_ref, gk_ref,
     kvbuf, kibuf, qraw, qrows, normb, wb, attn, wscore, iscore, lbuf, tbuf, l1, t1, l2, t2, lx, tx,
-    lall, tall, dbuf, dall, gwacc, gkbuf, gkrecv, hbuf,
+    lall, tall, dbuf, dall, gwacc, gkbuf, gkpair, gksum, gkrecv, hbuf,
     q_sem, ring_send, ring_recv, core_send, core_recv, s1_send, s1_recv, s2_send, s2_recv,
-    d_send, d_recv, gk_send, gk_recv, h_send, h_recv,
+    d_send, d_recv, gp_send, gp_recv, gk_send, gk_recv, h_send, h_recv,
 ):
     s = lax.axis_index("seq")
     h = lax.axis_index("head")
@@ -230,7 +230,19 @@
     swap.wait_recv()
 
     incoming = []
-    own = None
+    sums = []
+
+    def pass_on(slot, copy):
+        copy.wait_recv()
+        pair = gkbuf[slot, c].astype(F32) + gkpair[slot].astype(F32)
+        if slot == 0:
+            return pair
+        gksum[slot - 1] = pair.astype(BF16)
+        incoming.append((slot, remote(
+            gksum.at[slot - 1], gkrecv.at[slot - 1], gk_send.at[slot - 1],
+            gk_recv.at[slot - 1], (seq_off(offsets[slot]), h))))
+        return None
+
     for slot in order[::-1]:
         delta = jnp.concatenate([dbuf[0, slot], dbuf[1, slot]], axis=0)
         wide = jnp.dot(spread, delta, preferred_element_type=F32)
@@ -239,13 +251,13 @@
         part = jnp.where(rectified > 0, wide * wb[...], 0.0).astype(BF16)
         dall[:, slot * rows:(slot + 1) * rows] = part
         grad = lax.dot_general(part, qi_ref[...], (((0,), (0,)), ((), ())), preferred_element_type=F32)
-        if slot == 0:
-            own = grad
-        else:
-            gkbuf[slot - 1] = grad.astype(BF16)
-            incoming.append((slot, remote(
-                gkbuf.at[slot - 1], gkrecv.at[slot - 1], gk_send.at[slot - 1],
-                gk_recv.at[slot - 1], (seq_off(offsets[slot]), h))))
+        gkbuf[slot] = grad.astype(BF16).reshape(2, half, grad.shape[1])
+        sums.append((slot, remote(gkbuf.at[slot, other], gkpair.at[slot], gp_send.at[slot],
+                                  gp_recv.at[slot], (s, partner))))
+        if len(sums) > 3:
+            pass_on(*sums.pop(0))
+    for slot, copy in sums:
+        own = pass_on(slot, copy)
 
     keys = kibuf[...].reshape(n * rows, ki_ref.shape[2])
     gq_ref[...] = jnp.dot(dall[...], keys, preferred_element_type=F32)
@@ -255,16 +267,17 @@
     for slot, copy in incoming:
         copy.wait_recv()
         own = own + gkrecv[slot - 1].astype(F32)
-    hbuf[h] = own.astype(BF16)
+    hbuf[h // 2, c] = own.astype(BF16)
     swaps = []
     for r in range(1, m):
         peer = (h + r) % m
-        swaps.append(remote(hbuf.at[h], hbuf.at[h], h_send.at[r - 1], h_recv.at[r - 1], (s, peer)))
+        swaps.append(remote(hbuf.at[h // 2, c], hbuf.at[h // 2, c], h_send.at[r - 1],
+                            h_recv.at[r - 1], (s, peer)))
     for copy in swaps:
         copy.wait_recv()
-    result = hbuf[0].astype(F32)
-    for r in range(1, m):
-        result = result + hbuf[r].astype(F32)
+    result = hbuf[0].reshape(gk_ref.shape).astype(F32)
+    for r in range(1, m // 2):
+        result = result + hbuf[r].reshape(gk_ref.shape).astype(F32)
     gk_ref[...] = result
     for copy in pending:
         copy.wait_send()
@@ -301,11 +314,11 @@
             V((n, half, rows), F32), V((n, half, rows), F32),
             V((2, n, half, rows), BF16), V((rows * iheads, n * rows), BF16),
             V((rows * iheads, rows), F32),
-            V((n - 1, rows, idim), BF16), V((n - 1, rows, idim), BF16),
-            V((m, rows, idim), BF16),
+            V((n, 2, half, idim), BF16), V((n, half, idim), BF16), V((n - 1, half, idim), BF16),
+            V((n - 1, half, idim), BF16), V((m // 2, 2, half, idim), BF16),
             D((heads,)), D((n, pieces + 1)), D((n, pieces + 1)), D((n, pieces + 1)),
             D((n, pieces + 1)), D((n, 2)), D((n, 2)),
-            D((n, peers, 2)), D((n, peers, 2)), D((1,)), D((1,)),
+            D((n, peers, 2)), D((n, peers, 2)), D((1,)), D((1,)), D((n,)), D((n,)),
             D((n - 1,)), D((n - 1,)), D((m - 1,)), D((m - 1,)),
         ]
         vmem = pl.BlockSpec(memory_space=pltpu.VMEM)

time: 42.1 us -> 41.6 us (0.988)
  Pallas kernels: 41.3 us -> 40.8 us
    pallas_call x1, Pallas kernels: 39.6 us -> 39.1 us  [on_device(): pl.pallas_call(functools.partial(kernel, n, m, heads, iheads, span, piece...]
where the time goes in v4:
time: 41.6 us; the launch traced here: 41.4 us
  Pallas kernels  40.8 us (98%)
  between operations  0.64 us (2%)
    pallas_call x1, Pallas kernels, on_device(): pl.pallas_call(functools.partial(kernel, n, m, heads, iheads, span, piece...  39.1 us
    pallas_call x1, Pallas kernels, on_device(): pl.pallas_call(write_out, out_shape=tuple((jax.ShapeDtypeStruct(x.shape,...  1.69 us

profile of v4, /device:TPU:0, one launch (start us, length us, event | category | flops | bytes accessed | tf_op | source)
XLA Modules:
  0.0 41.4 jit_solution(10682568632729269972)
XLA Ops:
  0.6 39.1 %shard_map.94 = (f32[512,128]{1,0:T(8,128)}, f32[4,128]{1,0:T(4,128)}, f32[128,128]{1,0:T(8,128)}) custom-call(bf16[8,576,128]{2,1,0:T(8,128)(2,1)} %bitcast.10, bf16[2,288,128]{2,1,0:T(8,128)(2,1)} %bitcast.11, f32[8,128]{1,0:T(8,128)} %bitcast.14, bf16[512,128]{1,0:T(8,128)(2,1)} %bitcast.12, bf16[2,64,128]{2,1,0:T(8,128)(2,1)} %bitcast.13, ...), custom_call_target="tpu_custom_call" | custom-call | tf_op jit(solution)/shard_map/pallas_call | solution.py:325
  39.7 1.7 %shard_map.95 = (f32[512,128]{1,0:T(8,128)}, f32[4,128]{1,0:T(4,128)}, f32[128,128]{1,0:T(8,128)}) custom-call(f32[512,128]{1,0:T(8,128)} %get-tuple-element.9.gq_in, f32[4,128]{1,0:T(4,128)} %get-tuple-element.10.gw_in, f32[128,128]{1,0:T(8,128)} %get-tuple-element.11.gk_in), custom_call_target="tpu_custom_call" | custom-call | tf_op jit(solution)/shard_map/pallas_call | solution.py:343
